TPU v7x, 512 devices: a whole 4x8x8 slice. The times are simulated.
512 devices in a mesh: dp: 16 (over y, core), table: 32 (over x, z).
Axes of the slice: x: 4, y: 8, z: 8, core: 2. Of those that a mesh axis runs over, the one named last changes fastest.
Arguments:
- bag_slots: int32 [262144, 32], P(('dp', 'table')), may hold values from -1 to 3071
- labels: float32 [262144], P(('dp', 'table')), may hold values from 0 to 1
- cold_ids: int32 [512, 32, 32], P(('dp', 'table')), may hold values from 0 to 1023
- cold_count: int32 [512, 32], P(('dp', 'table')), may hold values from 1 to 32, 512 in all within a row
- table: float32 [32768, 256], P('table'), may hold values from -1.8 to 1.8
- adagrad_sum: float32 [32768], P('table'), may hold values from 0.1 to 10
- hot_ids: int32 [2048], P('table'), may hold values from 0 to 1023
- w_in: bfloat16 [256, 4096], replicated, may hold values from -0.375 to 0.375
- w_out: bfloat16 [4096], replicated, may hold values from -0.09375 to 0.09375
Outputs:
- new_table: float32 [32768, 256], P('table')
- new_sum: float32 [32768], P('table')
Inputs may be any that keep to these rules, and one draw needn't show every extreme that they name: `bag_slots`: -1 marks an empty bag entry. `cold_count`: each reader's counts sum to 512.
All inputs are finite; a program needn't handle non-finite values.
Results may differ from a plain program's by a relative error of at most 0.0045.
The roundings to bfloat16 on the way count: a program that leaves them out, or rounds other values in their place, can miss the bound.
Values may be sent and summed in bfloat16 or wider, within the bound.
A program may use at most 64 MiB of HBM per device.

v0:
```python
import jax
import jax.numpy as jnp
from jax import lax
from jax.sharding import PartitionSpec as P

learning_rate = 0.3


def adagrad_step(own_table, own_sum, grad):
    new_sum = own_sum + jnp.mean(grad * grad, axis=1)
    new_table = own_table - learning_rate * grad / jnp.sqrt(new_sum)[:, None]
    return (new_table, new_sum)


def per_device(bag_slots, labels, cold_ids, cold_count, table, adagrad_sum, hot_ids, w_in, w_out):
    owners = lax.axis_size("table")
    hot_dev = hot_ids.shape[0]
    slot_cap = cold_ids.shape[2]
    batch = bag_slots.shape[0]
    width = table.shape[1]
    hot_cols = owners * hot_dev
    vocab_size = owners * (hot_dev + slot_cap)
    table_bf = table.astype(jnp.bfloat16)
    hot_rows = table_bf[hot_ids]
    sample_ids = jnp.broadcast_to(jnp.arange(batch, dtype=jnp.int32)[:, None], bag_slots.shape)
    column_ids = jnp.where(bag_slots < 0, vocab_size, bag_slots)
    incidence = (
        jnp.zeros((batch, vocab_size), jnp.bfloat16)
        .at[sample_ids, column_ids]
        .add(jnp.ones(bag_slots.shape, jnp.bfloat16), mode="drop")
    )
    hot_incidence = incidence[:, :hot_cols]
    cold_incidence = incidence[:, hot_cols:]
    asked_ids = lax.all_to_all(cold_ids[0], "table", split_axis=0, concat_axis=0, tiled=True)
    served = table_bf[asked_ids]
    fetched = lax.all_to_all(served, "table", split_axis=0, concat_axis=0, tiled=True)
    live_mask = jnp.arange(slot_cap, dtype=jnp.int32)[None, :] < cold_count[0][:, None]
    fetched = jnp.where(live_mask[..., None], fetched, jnp.zeros_like(fetched))
    cold_pooled = jnp.dot(
        cold_incidence, fetched.reshape(-1, width), preferred_element_type=jnp.float32
    )
    columns = hot_incidence
    pooled = (
        cold_pooled
        + jnp.dot(
            columns,
            lax.all_gather(hot_rows, "table", axis=0, tiled=True),
            preferred_element_type=jnp.float32,
        )
    ).astype(jnp.bfloat16)
    pre_act = jnp.dot(pooled, w_in, preferred_element_type=jnp.float32)
    hidden = jax.nn.relu(pre_act).astype(jnp.bfloat16)
    logit = jnp.dot(hidden, w_out, preferred_element_type=jnp.float32)
    dlogit = jax.nn.sigmoid(logit) - labels
    dhidden = (dlogit[:, None] * w_out.astype(jnp.float32)[None, :] * (pre_act > 0)).astype(
        jnp.bfloat16
    )
    dpooled = lax.dot_general(
        dhidden, w_in, (((1,), (1,)), ((), ())), preferred_element_type=jnp.float32
    ).astype(jnp.bfloat16)
    columns = hot_incidence
    hot_grad = lax.psum_scatter(
        lax.dot_general(
            columns, dpooled, (((0,), (0,)), ((), ())), preferred_element_type=jnp.float32
        ).astype(jnp.bfloat16),
        "table",
        scatter_dimension=0,
        tiled=True,
    ).astype(jnp.float32)
    cold_term = lax.dot_general(
        cold_incidence, dpooled, (((0,), (0,)), ((), ())), preferred_element_type=jnp.float32
    )
    cold_term = jnp.where(live_mask[..., None], cold_term.reshape(owners, slot_cap, width), 0.0)
    returned = lax.all_to_all(
        cold_term.astype(jnp.bfloat16), "table", split_axis=0, concat_axis=0, tiled=True
    ).astype(cold_term.dtype)
    grad = jnp.zeros(table.shape, jnp.float32).at[hot_ids].add(hot_grad)
    grad = grad.at[asked_ids.reshape(-1)].add(returned.reshape(-1, width))
    total_grad = lax.psum(grad.astype(jnp.bfloat16), "dp").astype(jnp.float32)
    new_table, new_sum = adagrad_step(table, adagrad_sum, total_grad)
    return (new_table, new_sum)


def solution(mesh):
    placed = (
        P(("dp", "table"), None),
        P(("dp", "table")),
        P(("dp", "table"), None, None),
        P(("dp", "table"), None),
        P("table", None),
        P("table"),
        P("table"),
        P(),
        P(),
    )
    return jax.shard_map(
        per_device,
        mesh=mesh,
        in_specs=placed,
        out_specs=(P("table", None), P("table")),
        check_vma=False,
    )
```

profile of v0, /device:TPU:1, one launch (start us, length us, event | category | flops | bytes accessed | tf_op | source)
XLA Modules:
  0.0 546.6 jit_solution(1328954373111065597)
XLA Ops:
  7.2 0.0 copy-start
  7.2 0.0 all-gather.3.cloned.1.call-start
  7.2 1.4 convert_element_type.35
  8.6 0.0 copy-start.5
  8.7 0.0 copy-start.4
  8.7 0.7 compare_select_fusion.4
  9.4 1.3 gather_fusion.1
  10.7 0.0 copy-start.8
  10.7 0.0 all-gather.3.cloned.1.call-update
  10.7 22.3 %all_to_all.22 = s32[32,1,32]{2,1,0:T(1,128)S(1)} all-to-all(s32[32,1,32]{2,1,0:T(1,128)} %bitcast.24), channel_id=1, replica_groups=mesh['dp'=16,'table'=32] {'table'}, dimensions={0} | all-to-all | bytes 8192 | tf_op jit(solution)/shard_map/all_to_all | solution.py:34
  33.0 0.0 copy-start.9
  33.0 0.1 reshape.131
  33.1 5.0 gather_fusion
  38.1 3.9 all-to-all-start.1
  42.0 0.0 reduce-scatter.2.cloned.1.call-start
  42.0 0.0 copy-done.5
  42.1 0.0 copy-done.4
  42.1 0.0 copy-done.8
  42.1 0.1 multiply_reduce_fusion
  42.2 0.0 copy-done.9
  42.2 0.1 and_reduce_fusion
  42.3 0.1 copy.11
  42.5 0.1 reshape.161
  42.6 114.8 %scatter_custom_fusion.2 = bf16[1572864]{0:T(1024)(128)(2,1)} fusion(s32[16384]{0:T(1024)S(1)} %reshape.161, bf16[16384]{0:T(1024)(128)(2,1)S(1)} %broadcast.91, bf16[]{:T(256)} %constant.12.clone.1), kind=kCustom, calls=%fused_computation.17 | custom fusion | flops 16384 | bytes 3145730
  157.4 0.0 copy-start.10
  157.4 5.8 %reshape.126 = bf16[512,3072]{1,0:T(8,128)(2,1)} reshape(bf16[1572864]{0:T(1024)(128)(2,1)} %scatter_custom_fusion.2) | data formatting | bytes 6291456 | tf_op jit(solution)/shard_map/scatter-add | solution.py:30
  163.2 0.0 copy-done.10
  163.2 0.1 iota_compare_fusion
  163.3 0.0 all-to-all-done.1
  163.3 0.2 broadcast_select_fusion
  163.5 1.7 fusion.28
  165.2 0.0 all-gather.3.cloned.1.call-done
  165.2 0.0 copy-done
  165.2 7.9 %fusion.19 = f32[512,4096]{1,0:T(8,128)} fusion(bf16[256,4096]{1,0:T(8,128)(2,1)S(1)} %copy-done, f32[512,256]{1,0:T(8,128)S(1)} %fusion.28, bf16[2048,256]{1,0:T(8,128)(2,1)} %all-gather.3.cloned.1.call-done, bf16[512,3072]{1,0:T(8,128)(2,1)} %reshape.126), kind=kOutput, calls=%fused_computation.24 | convolution fusion | flops 1610874880 | bytes 14155776 | tf_op jit(solution)/shard_map/dot_general | solution.py:51
  173.2 0.0 copy-start.7
  173.2 0.0 copy-start.1
  173.2 4.7 fusion
  177.9 0.0 copy-done.7
  177.9 1.0 copy-done.1
  178.9 0.0 copy-start.2
  179.0 1.4 fusion.14
  180.4 0.5 copy-done.2
  180.8 1.8 convolution_convert_fusion
  182.6 0.0 reduce-scatter.2.cloned.1.call-update
  182.6 1.7 fusion.26
  184.3 1.0 select_convert_fusion.4
  185.3 0.0 copy-start.6
  185.3 9.5 %all-to-all-start.2 = ((bf16[32,32,256]{2,1,0:T(8,128)(2,1)}), bf16[32,32,256]{2,1,0:T(8,128)(2,1)}, u32[]{:S(2)}, u32[]{:S(2)}) async-start(bf16[32,32,256]{2,1,0:T(8,128)(2,1)} %select_convert_fusion.4), calls=%async_computation.3 | async-start | bytes 1048576 | tf_op jit(solution)/shard_map/all_to_all | solution.py:74
  194.8 0.0 all-reduce.2.cloned.1.call-start
  194.9 0.5 broadcast.113
  195.4 0.7 reduce.7
  196.1 0.1 reshape.119
  196.2 207.6 %reduce-scatter.2.cloned.1.call-done = bf16[64,256]{1,0:T(8,128)(2,1)} async-done(((bf16[2048,256]{1,0:T(8,128)(2,1)}), bf16[64,256]{1,0:T(8,128)(2,1)}) %reduce-scatter.2.cloned.1.call-update) | async-done | bytes 32784 | tf_op jit(solution)/shard_map/reduce_scatter | solution.py:62
  403.8 2.1 scatter_custom_fusion
  406.0 0.0 all-to-all-done.2
  406.0 8.6 %scatter_custom_fusion.1 = f32[1024,256]{1,0:T(8,128)} fusion(f32[1024,256]{1,0:T(8,128)} %scatter_custom_fusion, s32[1024]{0:T(1024)S(1)} %bitcast.26, bf16[1024,256]{1,0:T(8,128)(2,1)} %bitcast.10), kind=kCustom, calls=%fused_computation.28 | custom fusion | flops 524288 | bytes 1572864 | tf_op jit(solution)/shard_map/scatter-add | solution.py:78
  414.6 2.1 convert_element_type.44
  416.7 0.0 all-reduce.2.cloned.1.call-update
  416.7 119.2 %all-reduce.2.cloned.1.call-done = bf16[1024,256]{1,0:T(8,128)(2,1)} async-done(((bf16[1024,256]{1,0:T(8,128)(2,1)}), bf16[1024,256]{1,0:T(8,128)(2,1)}) %all-reduce.2.cloned.1.call-update) | async-done | bytes 524304 | tf_op jit(solution)/shard_map/psum | solution.py:79
  535.9 1.3 fusion.23
  537.2 0.0 copy-done.6
  537.2 0.6 fusion.36
  537.8 0.0 copy-done.3
  537.8 2.2 fusion.22
  (12 shorter events, 0.1 us)
Async XLA Ops:
  7.2 158.1 %copy-start = (bf16[256,4096]{1,0:T(8,128)(2,1)S(1)}, bf16[256,4096]{1,0:T(8,128)(2,1)}, u32[]{:S(2)}) copy-start(bf16[256,4096]{1,0:T(8,128)(2,1)} %param.16) | copy-start | bytes 6291460
  7.2 158.0 %all-gather.3.cloned.1.call-start = ((), (), s32[]{:S(2)}) async-start(), calls=%async_computation.6 | async-start | bytes 1081344 | tf_op jit(solution)/shard_map/all_gather | solution.py:47
  8.6 33.4 %copy-start.5 = (bf16[4096]{0:T(1024)(128)(2,1)S(1)}, bf16[4096]{0:T(1024)(128)(2,1)}, u32[]{:S(2)}) copy-start(bf16[4096]{0:T(1024)(128)(2,1)} %param.17) | copy-start | bytes 24580
  8.7 33.4 %copy-start.4 = (s32[512,32]{0,1:T(8,128)S(1)}, s32[512,32]{0,1:T(8,128)}, u32[]{:S(2)}) copy-start(s32[512,32]{0,1:T(8,128)} %param.9) | copy-start | bytes 196612
  10.7 31.4 %copy-start.8 = (s32[2]{0:T(128)S(1)}, s32[2]{0:T(128)}, u32[]{:S(2)}) copy-start(s32[2]{0:T(128)} %constant.6) | copy-start | bytes 28
  33.0 9.2 %copy-start.9 = (s32[2]{0:T(128)S(1)}, s32[2]{0:T(128)}, u32[]{:S(2)}) copy-start(s32[2]{0:T(128)} %constant.18) | copy-start | bytes 28
  38.1 125.2 %all-to-all-start.1 = ((bf16[32,32,256]{2,1,0:T(8,128)(2,1)}), bf16[32,32,256]{2,1,0:T(8,128)(2,1)S(1)}, u32[]{:S(2)}, u32[]{:S(2)}) async-start(bf16[32,32,256]{2,1,0:T(8,128)(2,1)} %bitcast.4), calls=%async_computation.1 | async-start | bytes 1048576 | tf_op jit(solution)/shard_map/all_to_all | solution.py:36
  42.0 361.8 %reduce-scatter.2.cloned.1.call-start = ((), (), s32[]{:S(2)}) async-start(), calls=%async_computation.4 | async-start | bytes 1081344 | tf_op jit(solution)/shard_map/reduce_scatter | solution.py:62
  157.4 5.8 %copy-start.10 = (s32[1,32]{1,0:T(1,128)S(1)}, s32[1,32]{1,0:T(1,128)}, u32[]{:S(2)}) copy-start(s32[1,32]{1,0:T(1,128)} %param.12) | copy-start | bytes 388
  173.2 4.7 copy-start.7
  173.2 5.8 %copy-start.1 = (f32[512,4096]{1,0:T(8,128)S(1)}, f32[512,4096]{1,0:T(8,128)}, u32[]{:S(2)}) copy-start(f32[512,4096]{1,0:T(8,128)} %fusion.19) | copy-start | bytes 25165828
  178.9 1.9 copy-start.2
  185.3 351.9 %copy-start.6 = (f32[1024]{0:T(1024)S(1)}, f32[1024]{0:T(1024)}, u32[]{:S(2)}) copy-start(f32[1024]{0:T(1024)} %param.14) | copy-start | bytes 12292
  185.3 352.5 %copy-start.3 = (f32[1024,256]{1,0:T(8,128)S(1)}, f32[1024,256]{1,0:T(8,128)}, u32[]{:S(2)}) copy-start(f32[1024,256]{1,0:T(8,128)} %param.13) | copy-start | bytes 3145732
  185.3 220.6 %all-to-all-start.2 = ((bf16[32,32,256]{2,1,0:T(8,128)(2,1)}), bf16[32,32,256]{2,1,0:T(8,128)(2,1)}, u32[]{:S(2)}, u32[]{:S(2)}) async-start(bf16[32,32,256]{2,1,0:T(8,128)(2,1)} %select_convert_fusion.4), calls=%async_computation.3 | async-start | bytes 1048576 | tf_op jit(solution)/shard_map/all_to_all | solution.py:74
  194.8 341.1 %all-reduce.2.cloned.1.call-start = ((), (), s32[]{:S(2)}) async-start(), calls=%async_computation.5 | async-start | bytes 1048576 | tf_op jit(solution)/shard_map/psum | solution.py:79
Sparse Core Ops, SparseCore 0:
  11.2 82.7 all-gather.2
  182.7 221.0 reduce-scatter.1
  416.8 119.0 all-reduce.1
where the time goes:
time: 547 us
  waiting for transfers between devices  327 us (60%)
  other arithmetic  136 us (25%)
  blocking collectives  22.3 us (4%)
  matrix products  19.2 us (4%)
  local copies, waits for them, and re-layouts  14.6 us (3%)
  between operations  14 us (3%)
  starting transfers between devices  13.5 us (2%)
    reduce_scatter x1, waiting for transfers between devices, per_device(): lax.psum_scatter(lax.dot_general(columns, dpooled, (((0,), (0,)), ((), ()...  208 us
    psum x1, waiting for transfers between devices, per_device(): total_grad = lax.psum(grad.astype(jnp.bfloat16), 'dp').astype(jnp.float32)  119 us
    unnamed x4, other arithmetic  115 us
    all_to_all x1, blocking collectives, per_device(): lax.all_to_all(cold_ids[0], 'table', split_axis=0, concat_axis=0, tiled=T...  22.3 us
  transfers between devices with their start and end apart: 5, of which 2 were waited for; matrix products, arithmetic and copies ran while one was open for 25% of the time, Pallas kernels for 0%

commit v1 on v0

--- a/solution.py
+++ b/solution.py
@@ -76,7 +76,9 @@
     ).astype(cold_term.dtype)
     grad = jnp.zeros(table.shape, jnp.float32).at[hot_ids].add(hot_grad)
     grad = grad.at[asked_ids.reshape(-1)].add(returned.reshape(-1, width))
-    total_grad = lax.psum(grad.astype(jnp.bfloat16), "dp").astype(jnp.float32)
+    total_grad = jnp.sum(lax.all_gather(grad.astype(jnp.bfloat16), "dp"), axis=0).astype(
+        jnp.float32
+    )
     new_table, new_sum = adagrad_step(table, adagrad_sum, total_grad)
     return (new_table, new_sum)
 

time: 547 us -> 491 us (0.90)
  waiting for transfers between devices: 327 us -> 271 us
    psum x1 -> x0, waiting for transfers between devices: 119 us -> none  [per_device(): total_grad = lax.psum(grad.astype(jnp.bfloat16), 'dp').astype(jnp.float32)]
    all_gather x0 -> x1, waiting for transfers between devices: none -> 61.8 us  [per_device(): lax.all_gather(grad.astype(jnp.bfloat16), 'dp')]
  transfers between devices with their start and end apart: 5 -> 5, of which waited for: 2 -> 2; matrix products, arithmetic and copies ran while one was open for 25% -> 27% of each run, Pallas kernels for 0% -> 0%
where the time goes in v1:
time: 491 us; the launch traced here: 490 us
  waiting for transfers between devices  271 us (55%)
  other arithmetic  136 us (28%)
  blocking collectives  22.3 us (5%)
  matrix products  19.2 us (4%)
  local copies, waits for them, and re-layouts  14.6 us (3%)
  between operations  14 us (3%)
  starting transfers between devices  13.4 us (3%)
    reduce_scatter x1, waiting for transfers between devices, per_device(): lax.psum_scatter(lax.dot_general(columns, dpooled, (((0,), (0,)), ((), ()...  209 us
    unnamed x4, other arithmetic  115 us
    all_gather x1, waiting for transfers between devices, per_device(): lax.all_gather(grad.astype(jnp.bfloat16), 'dp')  61.8 us
    all_to_all x1, blocking collectives, per_device(): lax.all_to_all(cold_ids[0], 'table', split_axis=0, concat_axis=0, tiled=T...  22.3 us
  transfers between devices with their start and end apart: 5, of which 2 were waited for; matrix products, arithmetic and copies ran while one was open for 27% of the time, Pallas kernels for 0%

profile of v1, /device:TPU:1, one launch (start us, length us, event | category | flops | bytes accessed | tf_op | source)
XLA Modules:
  0.0 490.3 jit_solution(13349649866934732644)
XLA Ops:
  7.2 0.0 copy-start
  7.2 0.0 all-gather.5.cloned.1.call-start
  7.2 1.4 convert_element_type.37
  8.6 0.0 copy-start.4
  8.7 0.0 copy-start.3
  8.7 0.7 compare_select_fusion.4
  9.4 1.3 gather_fusion.1
  10.7 0.0 copy-start.7
  10.7 0.0 all-gather.5.cloned.1.call-update
  10.7 22.3 %all_to_all.22 = s32[32,1,32]{2,1,0:T(1,128)S(1)} all-to-all(s32[32,1,32]{2,1,0:T(1,128)} %bitcast.26), channel_id=1, replica_groups=mesh['dp'=16,'table'=32] {'table'}, dimensions={0} | all-to-all | bytes 8192 | tf_op jit(solution)/shard_map/all_to_all | solution.py:34
  33.0 0.0 copy-start.8
  33.0 0.1 reshape.131
  33.1 5.0 %gather_fusion = bf16[1024,256]{1,0:T(8,128)(2,1)} fusion(bf16[1024,256]{1,0:T(8,128)(2,1)S(1)} %convert_element_type.37, s32[1024]{0:T(1024)S(1)} %broadcast_clamp_fusion), kind=kCustom, calls=%fused_computation | custom fusion | bytes 1052672 | tf_op jit(solution)/shard_map/gather | solution.py:35
  38.1 3.9 all-to-all-start.1
  42.0 0.0 reduce-scatter.2.cloned.1.call-start
  42.0 0.0 copy-done.4
  42.1 0.0 copy-done.3
  42.1 0.0 copy-done.7
  42.1 0.1 multiply_reduce_fusion
  42.2 0.0 copy-done.8
  42.2 0.1 and_reduce_fusion
  42.3 0.1 copy.12
  42.5 0.1 reshape.161
  42.6 114.8 %scatter_custom_fusion.2 = bf16[1572864]{0:T(1024)(128)(2,1)} fusion(s32[16384]{0:T(1024)S(1)} %reshape.161, bf16[16384]{0:T(1024)(128)(2,1)S(1)} %broadcast.91, bf16[]{:T(256)} %constant.12.clone.1), kind=kCustom, calls=%fused_computation.17 | custom fusion | flops 16384 | bytes 3145730
  157.4 0.0 copy-start.9
  157.4 5.8 %reshape.126 = bf16[512,3072]{1,0:T(8,128)(2,1)} reshape(bf16[1572864]{0:T(1024)(128)(2,1)} %scatter_custom_fusion.2) | data formatting | bytes 6291456 | tf_op jit(solution)/shard_map/scatter-add | solution.py:30
  163.2 0.0 copy-done.9
  163.2 0.1 iota_compare_fusion
  163.3 0.0 all-to-all-done.1
  163.3 0.2 broadcast_select_fusion
  163.5 1.7 fusion.28
  165.2 0.0 all-gather.5.cloned.1.call-done
  165.2 0.0 copy-done
  165.2 7.9 %fusion.19 = f32[512,4096]{1,0:T(8,128)} fusion(bf16[256,4096]{1,0:T(8,128)(2,1)S(1)} %copy-done, f32[512,256]{1,0:T(8,128)S(1)} %fusion.28, bf16[2048,256]{1,0:T(8,128)(2,1)} %all-gather.5.cloned.1.call-done, bf16[512,3072]{1,0:T(8,128)(2,1)} %reshape.126), kind=kOutput, calls=%fused_computation.24 | convolution fusion | flops 1610874880 | bytes 14155776 | tf_op jit(solution)/shard_map/dot_general | solution.py:51
  173.2 0.0 copy-start.6
  173.2 0.0 copy-start.1
  173.2 4.7 fusion
  177.9 0.0 copy-done.6
  177.9 1.0 copy-done.1
  178.9 0.0 copy-start.2
  179.0 1.4 fusion.14
  180.3 0.5 copy-done.2
  180.8 1.8 convolution_convert_fusion
  182.6 0.0 reduce-scatter.2.cloned.1.call-update
  182.6 1.7 fusion.26
  184.3 1.0 select_convert_fusion.4
  185.4 9.3 %all-to-all-start.2 = ((bf16[32,32,256]{2,1,0:T(8,128)(2,1)}), bf16[32,32,256]{2,1,0:T(8,128)(2,1)}, u32[]{:S(2)}, u32[]{:S(2)}) async-start(bf16[32,32,256]{2,1,0:T(8,128)(2,1)} %select_convert_fusion.4), calls=%async_computation.3 | async-start | bytes 1048576 | tf_op jit(solution)/shard_map/all_to_all | solution.py:74
  194.7 0.0 all-gather.7.cloned.1.call-start
  194.8 0.5 broadcast.113
  195.3 0.7 reduce.8
  196.0 0.1 reshape.119
  196.1 208.6 %reduce-scatter.2.cloned.1.call-done = bf16[64,256]{1,0:T(8,128)(2,1)} async-done(((bf16[2048,256]{1,0:T(8,128)(2,1)}), bf16[64,256]{1,0:T(8,128)(2,1)}) %reduce-scatter.2.cloned.1.call-update) | async-done | bytes 32784 | tf_op jit(solution)/shard_map/reduce_scatter | solution.py:62
  404.7 1.4 scatter_custom_fusion
  406.1 0.0 all-to-all-done.2
  406.1 6.9 %scatter_custom_fusion.1 = f32[1024,256]{1,0:T(8,128)S(1)} fusion(f32[1024,256]{1,0:T(8,128)S(1)} %scatter_custom_fusion, s32[1024]{0:T(1024)S(1)} %bitcast.28, bf16[1024,256]{1,0:T(8,128)(2,1)} %bitcast.11), kind=kCustom, calls=%fused_computation.28 | custom fusion | flops 524288 | bytes 1572864 | tf_op jit(solution)/shard_map/scatter-add | solution.py:78
  413.0 0.8 convert_element_type.46
  413.9 0.0 all-gather.7.cloned.1.call-update
  413.9 61.8 %all-gather.7.cloned.1.call-done = bf16[16384,256]{1,0:T(8,128)(2,1)} async-done(((bf16[1024,256]{1,0:T(8,128)(2,1)}), bf16[16384,256]{1,0:T(8,128)(2,1)}) %all-gather.7.cloned.1.call-update) | async-done | bytes 8388624 | tf_op jit(solution)/shard_map/all_gather | solution.py:79
  475.7 0.0 copy-start.5
  475.7 4.8 reduce_sum.21
  480.6 0.2 fusion.23
  480.8 0.0 copy-done.5
  480.8 0.6 fusion.36
  481.4 2.4 fusion.22
  (11 shorter events, 0.1 us)
Async XLA Ops:
  7.2 158.1 %copy-start = (bf16[256,4096]{1,0:T(8,128)(2,1)S(1)}, bf16[256,4096]{1,0:T(8,128)(2,1)}, u32[]{:S(2)}) copy-start(bf16[256,4096]{1,0:T(8,128)(2,1)} %param.16) | copy-start | bytes 6291460
  7.2 158.0 %all-gather.5.cloned.1.call-start = ((), (), s32[]{:S(2)}) async-start(), calls=%async_computation.5 | async-start | bytes 1081344 | tf_op jit(solution)/shard_map/all_gather | solution.py:47
  8.6 33.4 %copy-start.4 = (bf16[4096]{0:T(1024)(128)(2,1)S(1)}, bf16[4096]{0:T(1024)(128)(2,1)}, u32[]{:S(2)}) copy-start(bf16[4096]{0:T(1024)(128)(2,1)} %param.17) | copy-start | bytes 24580
  8.7 33.4 %copy-start.3 = (s32[512,32]{0,1:T(8,128)S(1)}, s32[512,32]{0,1:T(8,128)}, u32[]{:S(2)}) copy-start(s32[512,32]{0,1:T(8,128)} %param.9) | copy-start | bytes 196612
  10.7 31.4 %copy-start.7 = (s32[2]{0:T(128)S(1)}, s32[2]{0:T(128)}, u32[]{:S(2)}) copy-start(s32[2]{0:T(128)} %constant.7) | copy-start | bytes 28
  33.0 9.2 %copy-start.8 = (s32[2]{0:T(128)S(1)}, s32[2]{0:T(128)}, u32[]{:S(2)}) copy-start(s32[2]{0:T(128)} %constant.19) | copy-start | bytes 28
  38.1 125.2 %all-to-all-start.1 = ((bf16[32,32,256]{2,1,0:T(8,128)(2,1)}), bf16[32,32,256]{2,1,0:T(8,128)(2,1)S(1)}, u32[]{:S(2)}, u32[]{:S(2)}) async-start(bf16[32,32,256]{2,1,0:T(8,128)(2,1)} %bitcast.4), calls=%async_computation.1 | async-start | bytes 1048576 | tf_op jit(solution)/shard_map/all_to_all | solution.py:36
  42.0 362.7 %reduce-scatter.2.cloned.1.call-start = ((), (), s32[]{:S(2)}) async-start(), calls=%async_computation.4 | async-start | bytes 1081344 | tf_op jit(solution)/shard_map/reduce_scatter | solution.py:62
  157.4 5.8 %copy-start.9 = (s32[1,32]{1,0:T(1,128)S(1)}, s32[1,32]{1,0:T(1,128)}, u32[]{:S(2)}) copy-start(s32[1,32]{1,0:T(1,128)} %param.12) | copy-start | bytes 388
  173.2 4.7 copy-start.6
  173.2 5.8 %copy-start.1 = (f32[512,4096]{1,0:T(8,128)S(1)}, f32[512,4096]{1,0:T(8,128)}, u32[]{:S(2)}) copy-start(f32[512,4096]{1,0:T(8,128)} %fusion.19) | copy-start | bytes 25165828
  178.9 1.9 copy-start.2
  185.4 220.7 %all-to-all-start.2 = ((bf16[32,32,256]{2,1,0:T(8,128)(2,1)}), bf16[32,32,256]{2,1,0:T(8,128)(2,1)}, u32[]{:S(2)}, u32[]{:S(2)}) async-start(bf16[32,32,256]{2,1,0:T(8,128)(2,1)} %select_convert_fusion.4), calls=%async_computation.3 | async-start | bytes 1048576 | tf_op jit(solution)/shard_map/all_to_all | solution.py:74
  194.7 281.0 %all-gather.7.cloned.1.call-start = ((), (), s32[]{:S(2)}) async-start(), calls=%async_computation.6 | async-start | bytes 8912896 | tf_op jit(solution)/shard_map/all_gather | solution.py:79
  475.7 5.1 %copy-start.5 = (f32[1024]{0:T(1024)S(1)}, f32[1024]{0:T(1024)}, u32[]{:S(2)}) copy-start(f32[1024]{0:T(1024)} %param.14) | copy-start | bytes 12292
Sparse Core Ops, SparseCore 0:
  11.2 82.7 all-gather.4
  182.7 221.8 reduce-scatter.1
  414.0 61.6 all-gather.6
